TPU v7x, 256 devices: a whole 4x4x8 slice. The times are simulated.
256 devices in a mesh: shot: 16 (over z, y_hi), grid: 16 (over x, y_lo, core).
Axes of the slice: x: 4, y: 4 (y_hi: 2, y_lo: 2; y = y_hi * 2 + y_lo), z: 8, core: 2. Of those that a mesh axis runs over, the one named last changes fastest.
Arguments:
- residuals: bfloat16 [4096, 4, 2048], P('shot', None, 'grid'), may hold values from -6 to 6
- encoding: bfloat16 [16, 4096], P(None, 'shot'), may hold values from -0.125 to 0.125
- receiver_cells: int32 [3, 2048], replicated, may hold values from 0 to 255, as said below
- velocity_term: float32 [256, 128, 256], P('grid'), may hold values from 0.02 to 0.18
- field_before: float32 [16, 256, 128, 256], P('shot', 'grid'), may hold values from -6 to 6
- field_start: float32 [16, 256, 128, 256], P('shot', 'grid'), may hold values from -6 to 6
Outputs:
- field_last: float32 [16, 256, 128, 256], P('shot', 'grid')
- field_end: float32 [16, 256, 128, 256], P('shot', 'grid')
Inputs may be any that keep to these rules, and one draw needn't show every extreme that they name: `receiver_cells`: row 0 holds first-dimension cells below 256, row 1 second-dimension cells below 128, row 2 third-dimension cells below 8.
All inputs are finite; a program needn't handle non-finite values.
Results may differ from a plain program's by a relative error of at most 0.0003.
Values sent between devices are 32-bit elements; how exact they have to be, the bound alone decides.
A program may use at most 128 MiB of HBM per device.

v0:
```python
import jax
import jax.numpy as jnp
from jax import lax
from jax.sharding import PartitionSpec as P

coeffs = (-205.0 / 72.0, 8.0 / 5.0, -1.0 / 5.0, 8.0 / 315.0, -1.0 / 560.0)


def cut_along(shard, dim, length):
    before, after = (shard.shape[:dim], shard.shape[dim + 1 :])
    return jnp.moveaxis(shard.reshape(*before, length, -1, *after), dim, 0)


def sum_at_owner(shard, axis, dim):
    length = lax.axis_size(axis)
    blocks = lax.all_to_all(cut_along(shard, dim, length), axis, 0, 0, tiled=True)
    return jnp.sum(blocks, axis=0)


def joined_along(blocks, dim):
    lengths = list(blocks.shape[1:])
    lengths[dim] *= blocks.shape[0]
    return jnp.moveaxis(blocks, 0, dim).reshape(lengths)


def from_everyone(shard, axis):
    copies = jnp.broadcast_to(shard, (lax.axis_size(axis), *shard.shape))
    return lax.all_to_all(copies, axis, split_axis=0, concat_axis=0, tiled=True)


def gather_directly(shard, axis, dim):
    return joined_along(from_everyone(shard, axis), dim)


def extended_2(shard, sides, width):
    for axis, dim in sides:
        size, length = (lax.axis_size(axis), shard.shape[dim])
        up = [(i, (i + 1) % size) for i in range(size - 1)]
        down = [(j, i) for i, j in up]
        last = lax.slice_in_dim(shard, length - width, length, axis=dim)
        initial = lax.slice_in_dim(shard, 0, width, axis=dim)
        before = lax.ppermute(last, axis, up)
        after = lax.ppermute(initial, axis, down)
        shard = jnp.concatenate([before, shard, after], axis=dim)
    return shard


def laplace(extended):
    width = extended.shape[0] - 8
    center = extended[4 : 4 + width]
    padded = jnp.pad(center, ((0, 0), (4, 4), (4, 4)))
    rows = center.shape[1]
    depth = center.shape[2]
    total = 3.0 * coeffs[0] * center
    for shift in range(1, 5):
        along_x = extended[4 + shift : 4 + shift + width] + extended[4 - shift : 4 - shift + width]
        along_y = (
            padded[:, 4 + shift : 4 + shift + rows, 4 : 4 + depth]
            + padded[:, 4 - shift : 4 - shift + rows, 4 : 4 + depth]
        )
        along_z = (
            padded[:, 4 : 4 + rows, 4 + shift : 4 + shift + depth]
            + padded[:, 4 : 4 + rows, 4 - shift : 4 - shift + depth]
        )
        total = total + coeffs[shift] * (along_x + along_y + along_z)
    return total


def inject(field, start_x, cells, values):
    width, rows, depth = field.shape
    local_x = cells[0] - start_x
    inside = (local_x >= 0) & (local_x < width)
    flat = (local_x * rows + cells[1]) * depth + cells[2]
    flat = jnp.where(inside, flat, width * rows * depth)
    return field.reshape(-1).at[flat].add(values, mode="drop").reshape(field.shape)


def local(residuals, encoding, receiver_cells, velocity_term, field_before, field_start):
    shot_rows, samples, local_receivers = residuals.shape
    flat_data = residuals.reshape(shot_rows, samples * local_receivers)
    own_traces = sum_at_owner(
        jnp.dot(encoding, flat_data, preferred_element_type=jnp.float32), "shot", 0
    )
    own_traces = own_traces.reshape(samples, local_receivers)
    traces = gather_directly(own_traces, "grid", 1)
    width = velocity_term.shape[0]
    start_x = lax.axis_index("grid") * width
    previous = field_before[0]
    current = field_start[0]
    for step in range(samples):
        extended = extended_2(current, (("grid", 0),), 4)
        advanced = 2.0 * current - previous + velocity_term * laplace(extended)
        advanced = inject(advanced, start_x, receiver_cells, traces[samples - 1 - step])
        previous, current = (current, advanced)
    return (previous[None], current[None])


def solution(mesh):
    return jax.shard_map(
        local,
        mesh=mesh,
        in_specs=(
            P("shot", None, "grid"),
            P(None, "shot"),
            P(),
            P("grid", None, None),
            P("shot", "grid", None, None),
            P("shot", "grid", None, None),
        ),
        out_specs=(P("shot", "grid", None, None), P("shot", "grid", None, None)),
        check_vma=False,
    )
```

profile of v0, /device:TPU:1, one launch (start us, length us, event | category | flops | bytes accessed | tf_op | source)
XLA Modules:
  0.0 201.6 jit_solution(15603051145540493418)
XLA Ops:
  0.6 0.0 copy-start
  0.7 0.0 copy-start.5
  0.7 0.7 copy-done
  1.3 1.1 convolution_bitcast_fusion
  2.4 0.6 copy.8
  3.1 11.7 %all-to-all-start = ((f32[16,1,512]{2,1,0:T(1,128)}), f32[16,1,512]{2,1,0:T(1,128)S(1)}, u32[]{:S(2)}, u32[]{:S(2)}) async-start(f32[16,1,512]{2,1,0:T(1,128)} %copy.8), calls=%async_computation | async-start | bytes 65536 | tf_op jit(solution)/shard_map/all_to_all | solution.py:16
  14.8 2.2 %slice_bitcast_fusion.1 = (f32[4,128,256]{2,1,0:T(8,128)}, f32[4,128,256]{2,1,0:T(8,128)}) fusion(f32[1,16,128,256]{3,2,1,0:T(8,128)} %param.11), kind=kLoop, calls=%fused_computation.211 | loop fusion | bytes 2097152 | tf_op jit(solution)/shard_map/slice | solution.py:41
  17.1 2.9 %collective-permute-start = (f32[4,128,256]{2,1,0:T(8,128)}, f32[4,128,256]{2,1,0:T(8,128)S(1)}, u32[]{:S(2)}, u32[]{:S(2)}) collective-permute-start(f32[4,128,256]{2,1,0:T(8,128)} %get-tuple-element.14), channel_id=1, source_target_pairs={{1,0},{2,1},{3,2},{4,3},{5,4},{6,5},{7,6},{8,7},{9,8},{10,9},{11,1... | collective-permute-start | bytes 1572872 | tf_op jit(solution)/shard_map/ppermute | solution.py:43
  19.9 2.7 %collective-permute-start.1 = (f32[4,128,256]{2,1,0:T(8,128)}, f32[4,128,256]{2,1,0:T(8,128)S(1)}, u32[]{:S(2)}, u32[]{:S(2)}) collective-permute-start(f32[4,128,256]{2,1,0:T(8,128)} %get-tuple-element.15), channel_id=1, source_target_pairs={{0,1},{1,2},{2,3},{3,4},{4,5},{5,6},{6,7},{7,8},{8,9},{9,10},{10,1... | collective-permute-start | bytes 1572872 | tf_op jit(solution)/shard_map/ppermute | solution.py:42
  22.6 1.3 all-to-all-done
  24.0 0.6 broadcast_in_dim.15
  24.6 6.6 %all-to-all-start.1 = ((f32[16,4,128]{2,1,0:T(4,128)}), f32[16,4,128]{2,1,0:T(4,128)S(1)}, u32[]{:S(2)}, u32[]{:S(2)}) async-start(f32[16,4,128]{2,1,0:T(4,128)} %broadcast_in_dim.15), calls=%async_computation.1 | async-start | bytes 65536 | tf_op jit(solution)/shard_map/all_to_all | solution.py:28
  31.3 5.8 %all-to-all-done.1 = f32[16,4,128]{2,1,0:T(4,128)S(1)} async-done(((f32[16,4,128]{2,1,0:T(4,128)}), f32[16,4,128]{2,1,0:T(4,128)S(1)}, u32[]{:S(2)}, u32[]{:S(2)}) %all-to-all-start.1) | async-done | bytes 32800 | tf_op jit(solution)/shard_map/all_to_all | solution.py:28
  37.1 30.5 %fusion.8 = f32[16,128,256]{2,1,0:T(8,128)S(1)} fusion(f32[16,128,256]{2,1,0:T(8,128)S(1)} %copy-done.5, f32[16,128,256]{2,1,0:T(8,128)} %bitcast.38, f32[4,128,256]{2,1,0:T(8,128)S(1)} %collective-permute-done.1, f32[4,128,256]{2,1,0:T(8,128)S(1)} %collective-permute-done, f32[1,16,128,256]{3,2,1,0:T(8,128)} %param.10), kind=kLoop, calls=%fused_computation.88 | loop fusion | flops 21495808 | bytes 9437184 | tf_op jit(solution)/shard_map/add | solution.py:92
  67.7 1.1 copy.9
  68.8 12.3 %scatter_fusion = f32[524288]{0:T(1024)S(1)} fusion(f32[524288]{0:T(1024)S(1)} %bitcast.35, s32[2048]{0:T(1024)S(1)} %bitcast.44, f32[2048]{0:T(1024)S(1)} %bitcast.52), kind=kCustom, calls=%fused_computation | custom fusion | flops 2048 | bytes 32768 | tf_op jit(solution)/shard_map/scatter-add | solution.py:75
  81.1 0.1 fusion.118
  81.1 0.9 slice.486
  82.1 2.5 %collective-permute-start.3 = (f32[4,128,256]{2,1,0:T(8,128)}, f32[4,128,256]{2,1,0:T(8,128)}, u32[]{:S(2)}, u32[]{:S(2)}) collective-permute-start(f32[4,128,256]{2,1,0:T(8,128)} %slice.486), channel_id=1, source_target_pairs={{0,1},{1,2},{2,3},{3,4},{4,5},{5,6},{6,7},{7,8},{8,9},{9,10},{10,1... | collective-permute-start | bytes 1572872 | tf_op jit(solution)/shard_map/ppermute | solution.py:42
  84.6 0.1 slice.483
  84.7 2.6 %collective-permute-start.2 = (f32[4,128,256]{2,1,0:T(8,128)S(1)}, f32[4,128,256]{2,1,0:T(8,128)S(1)}, u32[]{:S(2)}, u32[]{:S(2)}) collective-permute-start(f32[4,128,256]{2,1,0:T(8,128)S(1)} %slice.483), channel_id=1, source_target_pairs={{1,0},{2,1},{3,2},{4,3},{5,4},{6,5},{7,6},{8,7},{9,8},{10,9},{11,1... | collective-permute-start | bytes 1572872 | tf_op jit(solution)/shard_map/ppermute | solution.py:43
  87.3 1.6 reshape.174
  89.0 7.7 %collective-permute-done.3 = f32[4,128,256]{2,1,0:T(8,128)} collective-permute-done((f32[4,128,256]{2,1,0:T(8,128)}, f32[4,128,256]{2,1,0:T(8,128)}, u32[]{:S(2)}, u32[]{:S(2)}) %collective-permute-start.3) | collective-permute-done | bytes 524320 | tf_op jit(solution)/shard_map/ppermute | solution.py:42
  96.6 1.1 constant_dynamic-update-slice_fusion.3
  97.7 0.0 copy-start.3
  97.7 0.0 copy-start.6
  97.7 2.2 %constant_dynamic-update-slice_fusion.1 = (f32[20,128,256]{2,1,0:T(8,128)S(1)}, f32[20,128,256]{2,1,0:T(8,128)S(1)}) fusion(f32[16,128,256]{2,1,0:T(8,128)} %reshape.174, f32[20,128,256]{2,1,0:T(8,128)S(1)} %constant_dynamic-update-slice_fusion.3), kind=kLoop, calls=%fused_computation.217 | loop fusion | bytes 6291456
  100.0 0.6 copy-done.6
  100.6 0.6 copy-done.10
  101.2 4.9 %fusion.44 = f32[16,128,256]{2,1,0:T(8,128)S(1)} fusion(f32[16,128,256]{2,1,0:T(8,128)S(1)} %copy-done.6, f32[16,128,256]{2,1,0:T(8,128)S(1)} %copy-done.3, f32[20,128,256]{2,1,0:T(8,128)S(1)} %get-tuple-element.13, f32[20,128,256]{2,1,0:T(8,128)S(1)} %constant_dynamic-update-slice_fusion, f32[1,16,128,256]{3,2,1,0:T(8,128)S(1)} %copy-done.10), kind=kLoop, calls=%fused_computation.124 | loop fusion | flops 17301504 | bytes 25165824 | tf_op jit(solution)/shard_map/add | solution.py:92
  106.1 1.1 copy.11
  107.2 12.3 %scatter_fusion.1 = f32[524288]{0:T(1024)S(1)} fusion(f32[524288]{0:T(1024)S(1)} %bitcast.36, s32[2048]{0:T(1024)S(1)} %bitcast.45, f32[2048]{0:T(1024)S(1)} %bitcast.51), kind=kCustom, calls=%fused_computation.1 | custom fusion | flops 2048 | bytes 32768 | tf_op jit(solution)/shard_map/scatter-add | solution.py:75
  119.4 0.1 fusion.117
  119.5 0.9 slice.515
  120.5 4.4 %collective-permute-start.5 = (f32[4,128,256]{2,1,0:T(8,128)}, f32[4,128,256]{2,1,0:T(8,128)}, u32[]{:S(2)}, u32[]{:S(2)}) collective-permute-start(f32[4,128,256]{2,1,0:T(8,128)} %slice.515), channel_id=1, source_target_pairs={{0,1},{1,2},{2,3},{3,4},{4,5},{5,6},{6,7},{7,8},{8,9},{9,10},{10,1... | collective-permute-start | bytes 1572872 | tf_op jit(solution)/shard_map/ppermute | solution.py:42
  124.9 0.1 slice.512
  125.0 2.1 %collective-permute-start.4 = (f32[4,128,256]{2,1,0:T(8,128)S(1)}, f32[4,128,256]{2,1,0:T(8,128)S(1)}, u32[]{:S(2)}, u32[]{:S(2)}) collective-permute-start(f32[4,128,256]{2,1,0:T(8,128)S(1)} %slice.512), channel_id=1, source_target_pairs={{1,0},{2,1},{3,2},{4,3},{5,4},{6,5},{7,6},{8,7},{9,8},{10,9},{11,1... | collective-permute-start | bytes 1572872 | tf_op jit(solution)/shard_map/ppermute | solution.py:43
  127.1 1.7 reshape.176
  128.8 8.1 %collective-permute-done.5 = f32[4,128,256]{2,1,0:T(8,128)} collective-permute-done((f32[4,128,256]{2,1,0:T(8,128)}, f32[4,128,256]{2,1,0:T(8,128)}, u32[]{:S(2)}, u32[]{:S(2)}) %collective-permute-start.5) | collective-permute-done | bytes 524320 | tf_op jit(solution)/shard_map/ppermute | solution.py:42
  136.9 1.1 constant_dynamic-update-slice_fusion.7
  138.0 0.0 copy-start.4
  138.0 2.2 %constant_dynamic-update-slice_fusion.5 = (f32[20,128,256]{2,1,0:T(8,128)S(1)}, f32[20,128,256]{2,1,0:T(8,128)S(1)}) fusion(f32[16,128,256]{2,1,0:T(8,128)} %reshape.176, f32[20,128,256]{2,1,0:T(8,128)S(1)} %constant_dynamic-update-slice_fusion.7), kind=kLoop, calls=%fused_computation.221 | loop fusion | bytes 6291456
  140.3 0.6 copy-done.4
  140.8 0.6 copy-done.7
  141.5 4.9 %fusion.70 = f32[16,128,256]{2,1,0:T(8,128)S(1)} fusion(f32[16,128,256]{2,1,0:T(8,128)S(1)} %copy-done.7, f32[16,128,256]{2,1,0:T(8,128)S(1)} %copy-done.1, f32[20,128,256]{2,1,0:T(8,128)S(1)} %get-tuple-element.9, f32[20,128,256]{2,1,0:T(8,128)S(1)} %constant_dynamic-update-slice_fusion.4, f32[16,128,256]{2,1,0:T(8,128)S(1)} %copy-done.4), kind=kLoop, calls=%fused_computation.150 | loop fusion | flops 17301504 | bytes 25165824 | tf_op jit(solution)/shard_map/add | solution.py:92
  146.3 1.1 copy.12
  147.4 12.3 %scatter_fusion.2 = f32[524288]{0:T(1024)S(1)} fusion(f32[524288]{0:T(1024)S(1)} %bitcast.34, s32[2048]{0:T(1024)S(1)} %bitcast.46, f32[2048]{0:T(1024)S(1)} %bitcast.50), kind=kCustom, calls=%fused_computation.2 | custom fusion | flops 2048 | bytes 32768 | tf_op jit(solution)/shard_map/scatter-add | solution.py:75
  159.7 0.1 fusion.116
  159.8 1.0 slice.544
  160.8 4.4 %collective-permute-start.7 = (f32[4,128,256]{2,1,0:T(8,128)}, f32[4,128,256]{2,1,0:T(8,128)}, u32[]{:S(2)}, u32[]{:S(2)}) collective-permute-start(f32[4,128,256]{2,1,0:T(8,128)} %slice.544), channel_id=1, source_target_pairs={{0,1},{1,2},{2,3},{3,4},{4,5},{5,6},{6,7},{7,8},{8,9},{9,10},{10,1... | collective-permute-start | bytes 1572872 | tf_op jit(solution)/shard_map/ppermute | solution.py:42
  165.1 0.1 slice.541
  165.3 1.9 collective-permute-start.6
  167.2 1.6 reshape.178
  168.9 1.6 broadcast_in_dim_reshape.6
  170.5 6.7 %collective-permute-done.7 = f32[4,128,256]{2,1,0:T(8,128)} collective-permute-done((f32[4,128,256]{2,1,0:T(8,128)}, f32[4,128,256]{2,1,0:T(8,128)}, u32[]{:S(2)}, u32[]{:S(2)}) %collective-permute-start.7) | collective-permute-done | bytes 524320 | tf_op jit(solution)/shard_map/ppermute | solution.py:42
  177.1 1.1 constant_dynamic-update-slice_fusion.11
  178.2 0.0 copy-start.8
  178.3 2.2 %constant_dynamic-update-slice_fusion.9 = (f32[20,128,256]{2,1,0:T(8,128)S(1)}, f32[20,128,256]{2,1,0:T(8,128)S(1)}) fusion(f32[16,128,256]{2,1,0:T(8,128)} %reshape.178, f32[20,128,256]{2,1,0:T(8,128)S(1)} %constant_dynamic-update-slice_fusion.11), kind=kLoop, calls=%fused_computation.225 | loop fusion | bytes 6291456
  180.5 0.6 copy-done.8
  181.1 0.6 copy-done.9
  181.7 4.9 %fusion.96 = f32[16,128,256]{2,1,0:T(8,128)S(1)} fusion(f32[16,128,256]{2,1,0:T(8,128)S(1)} %copy-done.8, f32[16,128,256]{2,1,0:T(8,128)S(1)} %copy-done.9, f32[20,128,256]{2,1,0:T(8,128)S(1)} %get-tuple-element.5, f32[20,128,256]{2,1,0:T(8,128)S(1)} %constant_dynamic-update-slice_fusion.8, f32[16,128,256]{2,1,0:T(8,128)S(1)} %copy-done.2), kind=kLoop, calls=%fused_computation.176 | loop fusion | flops 17301504 | bytes 25165824 | tf_op jit(solution)/shard_map/add | solution.py:92
  186.6 1.1 copy.13
  187.7 12.3 %scatter_fusion.3 = f32[524288]{0:T(1024)S(1)} fusion(f32[524288]{0:T(1024)S(1)} %bitcast.37, s32[2048]{0:T(1024)S(1)} %bitcast.47, f32[2048]{0:T(1024)S(1)} %bitcast.49), kind=kCustom, calls=%fused_computation.3 | custom fusion | flops 2048 | bytes 32768 | tf_op jit(solution)/shard_map/scatter-add | solution.py:75
  200.0 1.6 broadcast_in_dim_reshape.7
  (22 shorter events, 0.3 us)
Async XLA Ops:
  0.6 0.7 copy-start
  0.6 30.6 %copy-start.11 = (s32[3,2048]{1,0:T(4,128)S(1)}, s32[3,2048]{1,0:T(4,128)}, u32[]{:S(2)}) copy-start(s32[3,2048]{1,0:T(4,128)} %param.8) | copy-start | bytes 73732
  0.7 36.5 %copy-start.5 = (f32[16,128,256]{2,1,0:T(8,128)S(1)}, f32[16,128,256]{2,1,0:T(8,128)}, u32[]{:S(2)}) copy-start(f32[16,128,256]{2,1,0:T(8,128)} %param.9) | copy-start | bytes 6291460
  3.1 20.9 %all-to-all-start = ((f32[16,1,512]{2,1,0:T(1,128)}), f32[16,1,512]{2,1,0:T(1,128)S(1)}, u32[]{:S(2)}, u32[]{:S(2)}) async-start(f32[16,1,512]{2,1,0:T(1,128)} %copy.8), calls=%async_computation | async-start | bytes 65536 | tf_op jit(solution)/shard_map/all_to_all | solution.py:16
  17.1 20.0 %collective-permute-start = (f32[4,128,256]{2,1,0:T(8,128)}, f32[4,128,256]{2,1,0:T(8,128)S(1)}, u32[]{:S(2)}, u32[]{:S(2)}) collective-permute-start(f32[4,128,256]{2,1,0:T(8,128)} %get-tuple-element.14), channel_id=1, source_target_pairs={{1,0},{2,1},{3,2},{4,3},{5,4},{6,5},{7,6},{8,7},{9,8},{10,9},{11,1... | collective-permute-start | bytes 1572872 | tf_op jit(solution)/shard_map/ppermute | solution.py:43
  19.9 17.2 %collective-permute-start.1 = (f32[4,128,256]{2,1,0:T(8,128)}, f32[4,128,256]{2,1,0:T(8,128)S(1)}, u32[]{:S(2)}, u32[]{:S(2)}) collective-permute-start(f32[4,128,256]{2,1,0:T(8,128)} %get-tuple-element.15), channel_id=1, source_target_pairs={{0,1},{1,2},{2,3},{3,4},{4,5},{5,6},{6,7},{7,8},{8,9},{9,10},{10,1... | collective-permute-start | bytes 1572872 | tf_op jit(solution)/shard_map/ppermute | solution.py:42
  24.6 12.5 %all-to-all-start.1 = ((f32[16,4,128]{2,1,0:T(4,128)}), f32[16,4,128]{2,1,0:T(4,128)S(1)}, u32[]{:S(2)}, u32[]{:S(2)}) async-start(f32[16,4,128]{2,1,0:T(4,128)} %broadcast_in_dim.15), calls=%async_computation.1 | async-start | bytes 65536 | tf_op jit(solution)/shard_map/all_to_all | solution.py:28
  82.1 14.5 %collective-permute-start.3 = (f32[4,128,256]{2,1,0:T(8,128)}, f32[4,128,256]{2,1,0:T(8,128)}, u32[]{:S(2)}, u32[]{:S(2)}) collective-permute-start(f32[4,128,256]{2,1,0:T(8,128)} %slice.486), channel_id=1, source_target_pairs={{0,1},{1,2},{2,3},{3,4},{4,5},{5,6},{6,7},{7,8},{8,9},{9,10},{10,1... | collective-permute-start | bytes 1572872 | tf_op jit(solution)/shard_map/ppermute | solution.py:42
  84.7 15.2 %collective-permute-start.2 = (f32[4,128,256]{2,1,0:T(8,128)S(1)}, f32[4,128,256]{2,1,0:T(8,128)S(1)}, u32[]{:S(2)}, u32[]{:S(2)}) collective-permute-start(f32[4,128,256]{2,1,0:T(8,128)S(1)} %slice.483), channel_id=1, source_target_pairs={{1,0},{2,1},{3,2},{4,3},{5,4},{6,5},{7,6},{8,7},{9,8},{10,9},{11,1... | collective-permute-start | bytes 1572872 | tf_op jit(solution)/shard_map/ppermute | solution.py:43
  97.7 2.3 %copy-start.3 = (f32[16,128,256]{2,1,0:T(8,128)S(1)}, f32[16,128,256]{2,1,0:T(8,128)}, u32[]{:S(2)}) copy-start(f32[16,128,256]{2,1,0:T(8,128)} %reshape.174) | copy-start | bytes 6291460
  97.7 2.8 %copy-start.6 = (f32[16,128,256]{2,1,0:T(8,128)S(1)}, f32[16,128,256]{2,1,0:T(8,128)}, u32[]{:S(2)}) copy-start(f32[16,128,256]{2,1,0:T(8,128)} %param.9) | copy-start | bytes 6291460
  97.7 3.5 %copy-start.10 = (f32[1,16,128,256]{3,2,1,0:T(8,128)S(1)}, f32[1,16,128,256]{3,2,1,0:T(8,128)}, u32[]{:S(2)}) copy-start(f32[1,16,128,256]{3,2,1,0:T(8,128)} %param.11) | copy-start | bytes 6291460
  120.5 16.4 %collective-permute-start.5 = (f32[4,128,256]{2,1,0:T(8,128)}, f32[4,128,256]{2,1,0:T(8,128)}, u32[]{:S(2)}, u32[]{:S(2)}) collective-permute-start(f32[4,128,256]{2,1,0:T(8,128)} %slice.515), channel_id=1, source_target_pairs={{0,1},{1,2},{2,3},{3,4},{4,5},{5,6},{6,7},{7,8},{8,9},{9,10},{10,1... | collective-permute-start | bytes 1572872 | tf_op jit(solution)/shard_map/ppermute | solution.py:42
  125.0 15.2 %collective-permute-start.4 = (f32[4,128,256]{2,1,0:T(8,128)S(1)}, f32[4,128,256]{2,1,0:T(8,128)S(1)}, u32[]{:S(2)}, u32[]{:S(2)}) collective-permute-start(f32[4,128,256]{2,1,0:T(8,128)S(1)} %slice.512), channel_id=1, source_target_pairs={{1,0},{2,1},{3,2},{4,3},{5,4},{6,5},{7,6},{8,7},{9,8},{10,9},{11,1... | collective-permute-start | bytes 1572872 | tf_op jit(solution)/shard_map/ppermute | solution.py:43
  138.0 2.3 %copy-start.1 = (f32[16,128,256]{2,1,0:T(8,128)S(1)}, f32[16,128,256]{2,1,0:T(8,128)}, u32[]{:S(2)}) copy-start(f32[16,128,256]{2,1,0:T(8,128)} %reshape.176) | copy-start | bytes 6291460
  138.0 2.8 %copy-start.4 = (f32[16,128,256]{2,1,0:T(8,128)S(1)}, f32[16,128,256]{2,1,0:T(8,128)}, u32[]{:S(2)}) copy-start(f32[16,128,256]{2,1,0:T(8,128)} %reshape.174) | copy-start | bytes 6291460
  138.0 3.5 %copy-start.7 = (f32[16,128,256]{2,1,0:T(8,128)S(1)}, f32[16,128,256]{2,1,0:T(8,128)}, u32[]{:S(2)}) copy-start(f32[16,128,256]{2,1,0:T(8,128)} %param.9) | copy-start | bytes 6291460
  160.8 16.4 %collective-permute-start.7 = (f32[4,128,256]{2,1,0:T(8,128)}, f32[4,128,256]{2,1,0:T(8,128)}, u32[]{:S(2)}, u32[]{:S(2)}) collective-permute-start(f32[4,128,256]{2,1,0:T(8,128)} %slice.544), channel_id=1, source_target_pairs={{0,1},{1,2},{2,3},{3,4},{4,5},{5,6},{6,7},{7,8},{8,9},{9,10},{10,1... | collective-permute-start | bytes 1572872 | tf_op jit(solution)/shard_map/ppermute | solution.py:42
  165.3 15.2 %collective-permute-start.6 = (f32[4,128,256]{2,1,0:T(8,128)S(1)}, f32[4,128,256]{2,1,0:T(8,128)S(1)}, u32[]{:S(2)}, u32[]{:S(2)}) collective-permute-start(f32[4,128,256]{2,1,0:T(8,128)S(1)} %slice.541), channel_id=1, source_target_pairs={{1,0},{2,1},{3,2},{4,3},{5,4},{6,5},{7,6},{8,7},{9,8},{10,9},{11,1... | collective-permute-start | bytes 1572872 | tf_op jit(solution)/shard_map/ppermute | solution.py:43
  178.2 2.3 %copy-start.2 = (f32[16,128,256]{2,1,0:T(8,128)S(1)}, f32[16,128,256]{2,1,0:T(8,128)}, u32[]{:S(2)}) copy-start(f32[16,128,256]{2,1,0:T(8,128)} %reshape.176) | copy-start | bytes 6291460
  178.2 2.8 %copy-start.8 = (f32[16,128,256]{2,1,0:T(8,128)S(1)}, f32[16,128,256]{2,1,0:T(8,128)}, u32[]{:S(2)}) copy-start(f32[16,128,256]{2,1,0:T(8,128)} %param.9) | copy-start | bytes 6291460
  178.2 3.5 %copy-start.9 = (f32[16,128,256]{2,1,0:T(8,128)S(1)}, f32[16,128,256]{2,1,0:T(8,128)}, u32[]{:S(2)}) copy-start(f32[16,128,256]{2,1,0:T(8,128)} %reshape.178) | copy-start | bytes 6291460
where the time goes:
time: 202 us
  other arithmetic  94.3 us (47%)
  starting transfers between devices  41.8 us (21%)
  local copies, waits for them, and re-layouts  33.7 us (17%)
  waiting for transfers between devices  29.6 us (15%)
    scatter-add x4, other arithmetic, inject(): field.reshape(-1).at[flat].add(values, mode='drop').reshape(field.shape)  49.1 us
    add x4, other arithmetic, local(): advanced = 2.0 * current - previous + velocity_term * laplace(extended)  45.1 us
    ppermute x4, waiting for transfers between devices, extended_2(): before = lax.ppermute(last, axis, up)  22.5 us
    unnamed x34, local copies, waits for them, and re-layouts  18.4 us
    ppermute x4, starting transfers between devices, extended_2(): before = lax.ppermute(last, axis, up)  14 us
    all_to_all x1, starting transfers between devices, sum_at_owner(): lax.all_to_all(cut_along(shard, dim, length), axis, 0, 0, tiled=True)  11.7 us
    ppermute x4, starting transfers between devices, extended_2(): after = lax.ppermute(initial, axis, down)  9.47 us
    all_to_all x1, starting transfers between devices, from_everyone(): return lax.all_to_all(copies, axis, split_axis=0, concat_axis=0, tiled=True)  6.63 us
  transfers between devices with their start and end apart: 10, of which 5 were waited for; matrix products, arithmetic and copies ran while one was open for 10% of the time, Pallas kernels for 0%

commit v1 on v0

v1 whole, which is shorter than its diff:
```python
import functools

import jax
import jax.numpy as jnp
from jax import lax
from jax.experimental import pallas as pl
from jax.experimental.pallas import tpu as pltpu
from jax.sharding import PartitionSpec as P

C0, C1, C2, C3, C4 = (-205.0 / 72.0, 8.0 / 5.0, -1.0 / 5.0, 8.0 / 315.0, -1.0 / 560.0)
SCALE = 5040.0
BAND = (8064.0, -1008.0, 128.0, -9.0)
MESH = pl.DeviceIdType.MESH
F32 = jnp.float32
BF16 = jnp.bfloat16


def band_of(distance):
    value = jnp.zeros(distance.shape, F32)
    for j, weight in enumerate(BAND, 1):
        value = jnp.where(distance == j, weight, value)
    return value.astype(BF16)


def iota(shape, dim):
    return lax.broadcasted_iota(jnp.int32, shape, dim)


def split(value):
    high = value.astype(BF16)
    return high, (value - high.astype(F32)).astype(BF16)


def dot(a, b):
    return jnp.dot(a, b, preferred_element_type=F32)


def kernel(
    n_grid, n_shot, res_hbm, enc_hbm, cells_hbm, vt_hbm, before_hbm, start_hbm, last_hbm, end_hbm,
    fa, fb, vt, halo, zmat, ymat, res, enc, cells, part, other, shots, traces, oy, oxz, inj,
    load_sem, out_sem, send_sem, recv_sem, pair_sem, shot_send, shot_recv, grid_send, grid_recv, ready,
):
    g = lax.axis_index("grid")
    s = lax.axis_index("shot")
    width, rows, depth = vt.shape
    half = depth // 2
    even = lax.rem(g, 2) == 0
    odd = lax.rem(g, 2) == 1
    has = (g > 0, g < n_grid - 1)
    near = (jnp.maximum(g - 1, 0), jnp.minimum(g + 1, n_grid - 1))
    pair = g // 2

    loads = [
        pltpu.make_async_copy(src, dst, load_sem.at[i])
        for i, (src, dst) in enumerate((
            (res_hbm, res),
            (enc_hbm, enc),
            (start_hbm.at[0], fb.at[pl.ds(4, width)]),
            (before_hbm.at[0], fa.at[pl.ds(4, width)]),
            (vt_hbm, vt),
            (cells_hbm, cells),
        ))
    ]
    for load in loads:
        load.start()

    barrier = pltpu.get_barrier_semaphore()

    def greet(**device):
        pl.semaphore_signal(barrier, inc=1, device_id=device, device_id_type=MESH)

    @pl.when(even)
    def _():
        greet(grid=near[1])

        @pl.when(has[0])
        def _():
            greet(grid=near[0])

        for k in range(1, n_shot):
            greet(shot=lax.rem(s + k, n_shot))
        for k in range(2, n_grid, 2):
            greet(grid=lax.rem(g + k, n_grid))

    @pl.when(odd)
    def _():
        for k in range(1, n_grid, 2):
            greet(grid=lax.rem(g + k, n_grid))

    zmat[...] = band_of(jnp.abs(iota((depth, depth), 0) - iota((depth, depth), 1)))
    ymat[...] = band_of(jnp.abs(iota((rows, 2 * rows), 0) - lax.rem(iota((rows, 2 * rows), 1), rows)))
    for f in (fa, fb):
        for p in (0, width + 4):
            f[pl.ds(p, 4)] = jnp.zeros((4, rows, depth), F32)

    def halo_copy(n, side, h, src):
        lanes = pl.ds(h * half, half)
        return pltpu.make_async_remote_copy(
            src_ref=src.at[:, :, lanes],
            dst_ref=halo.at[n, 1 - side, :, :, lanes],
            send_sem=send_sem.at[n, side, h],
            recv_sem=recv_sem.at[n, 1 - side, h],
            device_id={"grid": near[side]},
            device_id_type=MESH,
        )

    def edge_of(n, side):
        if n == 0:
            return start_hbm.at[0, pl.ds(0 if side == 0 else width - 4, 4)]
        f = fb if n % 2 == 0 else fa
        return f.at[pl.ds(4 if side == 0 else width, 4)]

    def send_halo(n, side, h):
        @pl.when(has[side])
        def _():
            halo_copy(n, side, h, edge_of(n, side)).start()

    def wait_sent(n):
        for side in (0, 1):
            @pl.when(has[side])
            def _():
                for h in (1, 0):
                    halo_copy(n, side, h, edge_of(n, side)).wait_send()

    def pair_copy(target):
        return pltpu.make_async_remote_copy(
            src_ref=part, dst_ref=other, send_sem=pair_sem.at[0], recv_sem=pair_sem.at[1],
            device_id={"grid": target}, device_id_type=MESH,
        )

    @pl.when(odd)
    def _():
        pl.semaphore_wait(barrier, jnp.where(has[1], 2, 1))
        for side in (0, 1):
            @pl.when(has[side])
            def _():
                pl.semaphore_signal(ready.at[1 - side], inc=1, device_id={"grid": near[side]}, device_id_type=MESH)

    for side in (1, 0):
        @pl.when(even & has[side])
        def _():
            pl.semaphore_wait(ready.at[side], 1)
    for h in (1, 0):
        for side in (0, 1):
            send_halo(0, side, h)

    loads[0].wait()
    loads[1].wait()
    shot_rows, samples = res.shape[0] // 4, 4
    core = lax.rem(g, 2)
    r = iota((8 * n_shot, n_shot), 0)
    pick = jnp.where(r // 8 == iota((8 * n_shot, n_shot), 1), 1.0, 0.0).astype(BF16)
    spread = jnp.where(
        iota((shot_rows, 4 * shot_rows), 0) == iota((shot_rows, 4 * shot_rows), 1) // 4, 1.0, 0.0
    ).astype(BF16)
    weights = dot(dot(pick, enc[...]).astype(BF16), spread)
    wide = (8 * n_shot, 4 * shot_rows)
    weights = jnp.where(lax.rem(iota(wide, 0), 8) - 4 * core == lax.rem(iota(wide, 1), 4), weights, 0.0)
    part[...] = dot(weights.astype(BF16), res[...]).reshape(n_shot, 8, 128)

    @pl.when(odd)
    def _():
        pair_copy(near[0]).start()

    for load in loads[2:]:
        load.wait()

    n_rec = cells.shape[1]
    oy[...] = jnp.where(iota((rows, n_rec), 0) == cells[1:2, :], 1.0, 0.0).astype(BF16)
    spot = (cells[0:1, :] - g * width) * 8 + cells[2:3, :]
    oxz[...] = jnp.where(iota((8 * width, n_rec), 0) == spot, 1.0, 0.0).astype(BF16)

    def own_part(n):
        cur, nxt = (fb, fa) if n % 2 == 0 else (fa, fb)

        def plane(x, carry):
            u = cur[x + 4]
            high, low = split(u)
            across = dot(jnp.concatenate([high, low], axis=1), jnp.concatenate([zmat[...], zmat[...]], axis=0))
            across = across + dot(ymat[...], jnp.concatenate([high, low], axis=0))
            total = (3.0 * C0) * u + across * (1.0 / SCALE)
            for j, weight in enumerate((C1, C2, C3, C4), 1):
                total = total + weight * (cur[x + 4 + j] + cur[x + 4 - j])
            nxt[x + 4] = 2.0 * u - nxt[x + 4] + vt[x] * total
            return carry

        lax.fori_loop(0, width, plane, 0)

    def add_halo(n, side, h):
        nxt = fa if n % 2 == 0 else fb
        lanes = pl.ds(h * half, half)

        @pl.when(has[side])
        def _():
            halo_copy(n, 1 - side, h, edge_of(n, 1 - side)).wait_recv()
            layer = [halo[n, side, 4 - d if side == 0 else d - 1, :, lanes] for d in (1, 2, 3, 4)]
            for i in range(4):
                x = i if side == 0 else width - 1 - i
                total = C4 * layer[3 - i]
                for j, weight in ((1, C1), (2, C2), (3, C3)):
                    if j > i:
                        total = total + weight * layer[j - i - 1]
                nxt[x + 4, :, lanes] = nxt[x + 4, :, lanes] + vt[x, :, lanes] * total

    def inject(n, planes):
        nxt = fa if n % 2 == 0 else fb
        lane = iota((rows, half), 1)
        values = inj[3 - n]
        for x in planes:
            moved = values if x == 0 else pltpu.roll(values, half - 8 * x, 1)
            nxt[x + 4, :, pl.ds(0, half)] = nxt[x + 4, :, pl.ds(0, half)] + jnp.where(lane < 8, moved, 0.0)

    edges = list(range(4)) + list(range(width - 4, width))
    inner = list(range(4, width - 4))

    own_part(0)

    def shot_copy(k):
        return pltpu.make_async_remote_copy(
            src_ref=part.at[k], dst_ref=shots.at[s], send_sem=shot_send.at[k], recv_sem=shot_recv.at[s],
            device_id={"shot": k}, device_id_type=MESH,
        )

    def shot_arrival(k):
        return pltpu.make_async_remote_copy(
            src_ref=part.at[k], dst_ref=shots.at[k], send_sem=shot_send.at[k], recv_sem=shot_recv.at[k],
            device_id={"shot": k}, device_id_type=MESH,
        )

    def grid_copy(target):
        return pltpu.make_async_remote_copy(
            src_ref=traces.at[pair], dst_ref=traces.at[pair], send_sem=grid_send.at[target], recv_sem=grid_recv.at[pair],
            device_id={"grid": target}, device_id_type=MESH,
        )

    def grid_arrival(e):
        return pltpu.make_async_remote_copy(
            src_ref=traces.at[e], dst_ref=traces.at[e], send_sem=grid_send.at[e], recv_sem=grid_recv.at[e],
            device_id={"grid": 2 * e}, device_id_type=MESH,
        )

    @pl.when(even)
    def _():
        pair_copy(near[1]).wait_recv()
        part[...] = part[...] + other[...]
        shots[s] = part[s]
        pl.semaphore_wait(barrier, n_shot - 1 + n_grid - 1)
        for i in range(1, n_shot):
            shot_copy(lax.rem(s + i, n_shot)).start()

    for side in (0, 1):
        add_halo(0, side, 1)
        send_halo(1, side, 1)

    @pl.when(even)
    def _():
        for i in range(1, n_shot):
            shot_arrival(lax.rem(s + i, n_shot)).wait_recv()
        traces[pair] = jnp.sum(shots[...], axis=0)
        for i in range(1, n_grid):
            grid_copy(lax.rem(g + i, n_grid)).start()

    for i in range(n_grid // 2):
        @pl.when(jnp.logical_not(even & (pair == i)))
        def _():
            grid_arrival(i).wait_recv()

    for t in range(4):
        row = jnp.concatenate([traces[i // 2, pl.ds(4 * (i % 2) + t, 1), :] for i in range(n_grid)], axis=1)
        total = jnp.zeros((rows, 8 * width), F32)
        for piece in split(row):
            scaled = oy[...] * jnp.broadcast_to(piece, oy.shape)
            total = total + lax.dot_general(scaled, oxz[...], (((1,), (1,)), ((), ())), preferred_element_type=F32)
        inj[t] = total

    inject(0, edges)
    for side in (0, 1):
        add_halo(0, side, 0)
        send_halo(1, side, 0)
    inject(0, inner)

    outs = []

    def put(f, out, at, length, lanes, sem):
        copy = pltpu.make_async_copy(
            f.at[pl.ds(at + 4, length), :, lanes], out.at[0, pl.ds(at, length), :, lanes], out_sem.at[sem]
        )
        copy.start()
        outs.append(copy)

    for n in (1, 2, 3):
        wait_sent(n - 1)
        own_part(n)
        inject(n, edges)
        if n == 3:
            inject(n, inner)
            put(fb, end_hbm, 4, width - 8, pl.ds(0, depth), 1)
        for h in (1, 0):
            for side in (0, 1):
                add_halo(n, side, h)
                if n < 3:
                    send_halo(n + 1, side, h)
                else:
                    put(fb, end_hbm, 0 if side == 0 else width - 4, 4, pl.ds(h * half, half), 2 + 2 * h + side)
        if n < 3:
            inject(n, inner)
        if n == 2:
            put(fa, last_hbm, 0, width, pl.ds(0, depth), 0)

    wait_sent(3)
    for copy in outs:
        copy.wait()

    @pl.when(odd)
    def _():
        pair_copy(near[0]).wait_send()

    @pl.when(even)
    def _():
        for i in range(1, n_shot):
            shot_copy(lax.rem(s + i, n_shot)).wait_send()
        for i in range(1, n_grid):
            grid_copy(lax.rem(g + i, n_grid)).wait_send()


def local(n_grid, n_shot, residuals, encoding, receiver_cells, velocity_term, field_before, field_start):
    shot_rows, samples, local_receivers = residuals.shape
    width, rows, depth = velocity_term.shape
    flat = residuals.reshape(shot_rows * samples, local_receivers)
    n_rec = receiver_cells.shape[1]
    any_space = pl.BlockSpec(memory_space=pl.ANY)
    dma = pltpu.SemaphoreType.DMA
    field = jax.ShapeDtypeStruct(field_start.shape, F32)
    return pl.pallas_call(
        functools.partial(kernel, n_grid, n_shot),
        out_shape=(field, field),
        in_specs=[pl.BlockSpec(memory_space=pltpu.HBM)] * 6,
        out_specs=(any_space, any_space),
        scratch_shapes=[
            pltpu.VMEM((width + 8, rows, depth), F32),
            pltpu.VMEM((width + 8, rows, depth), F32),
            pltpu.VMEM((width, rows, depth), F32),
            pltpu.VMEM((4, 2, 4, rows, depth), F32),
            pltpu.VMEM((depth, depth), BF16),
            pltpu.VMEM((rows, 2 * rows), BF16),
            pltpu.VMEM(flat.shape, BF16),
            pltpu.VMEM(encoding.shape, BF16),
            pltpu.VMEM(receiver_cells.shape, jnp.int32),
            pltpu.VMEM((n_shot, 8, local_receivers), F32),
            pltpu.VMEM((n_shot, 8, local_receivers), F32),
            pltpu.VMEM((n_shot, 8, local_receivers), F32),
            pltpu.VMEM((n_grid // 2, 8, local_receivers), F32),
            pltpu.VMEM((rows, n_rec), BF16),
            pltpu.VMEM((8 * width, n_rec), BF16),
            pltpu.VMEM((4, rows, 8 * width), F32),
            dma((6,)),
            dma((6,)),
            dma((4, 2, 2)),
            dma((4, 2, 2)),
            dma((2,)),
            dma((n_shot,)),
            dma((n_shot,)),
            dma((n_grid,)),
            dma((n_grid // 2,)),
            pltpu.SemaphoreType.REGULAR((2,)),
        ],
        compiler_params=pltpu.CompilerParams(
            collective_id=0, has_side_effects=True, vmem_limit_bytes=48 * 1024 * 1024
        ),
        name="window",
    )(flat, encoding, receiver_cells, velocity_term, field_before, field_start)


def solution(mesh):
    return jax.shard_map(
        functools.partial(local, mesh.shape["grid"], mesh.shape["shot"]),
        mesh=mesh,
        in_specs=(
            P("shot", None, "grid"),
            P(None, "shot"),
            P(),
            P("grid", None, None),
            P("shot", "grid", None, None),
            P("shot", "grid", None, None),
        ),
        out_specs=(P("shot", "grid", None, None), P("shot", "grid", None, None)),
        check_vma=False,
    )
```

time: 202 us -> 66.6 us (0.33)
  other arithmetic: 94.3 us -> 0 us
  Pallas kernels: 0 us -> 60.7 us
  starting transfers between devices: 41.8 us -> 0 us
  waiting for transfers between devices: 29.6 us -> 0 us
  local copies, waits for them, and re-layouts: 33.7 us -> 5.04 us
    pallas_call x0 -> x1, Pallas kernels: none -> 60.7 us  [local(): pl.pallas_call(functools.partial(kernel, n_grid, n_shot), out_shape=(fiel...]
    scatter-add x4 -> x0, other arithmetic: 49.1 us -> none  [inject(): field.reshape(-1).at[flat].add(values, mode='drop').reshape(field.shape)]
    add x4 -> x0, other arithmetic: 45.1 us -> none  [local(): advanced = 2.0 * current - previous + velocity_term * laplace(extended)]
    ppermute x8 -> x0, starting transfers between devices: 23.4 us -> none  [the longest x4 14 us: extended_2(): before = lax.ppermute(last, axis, up)]
    ppermute x8 -> x0, waiting for transfers between devices: 22.5 us -> none  [the longest x4 22.5 us: extended_2(): before = lax.ppermute(last, axis, up)]
    all_to_all x2 -> x0, starting transfers between devices: 18.4 us -> none  [the longest x1 11.7 us: sum_at_owner(): lax.all_to_all(cut_along(shard, dim, length), axis, 0, 0, tiled=True)]
    unnamed x34 -> x8, local copies, waits for them, and re-layouts: 18.4 us -> 5.04 us
    all_to_all x2 -> x0, waiting for transfers between devices: 7.08 us -> none  [the longest x1 5.77 us: from_everyone(): return lax.all_to_all(copies, axis, split_axis=0, concat_axis=0, tiled=True)]
  transfers between devices with their start and end apart: 10 -> 0, of which waited for: 5 -> 0; matrix products, arithmetic and copies ran while one was open for 10% -> 0% of each run, Pallas kernels for 0% -> 0%
where the time goes in v1:
time: 66.6 us; the launch traced here: 66.4 us
  Pallas kernels  60.7 us (91%)
  local copies, waits for them, and re-layouts  5.04 us (8%)
    pallas_call x1, Pallas kernels, local(): pl.pallas_call(functools.partial(kernel, n_grid, n_shot), out_shape=(fiel...  60.7 us
    unnamed x8, local copies, waits for them, and re-layouts  5.04 us

profile of v1, /device:TPU:1, one launch (start us, length us, event | category | flops | bytes accessed | tf_op | source)
XLA Modules:
  0.0 66.4 jit_solution(14172503140758114913)
XLA Ops:
  0.6 0.0 copy-start
  0.6 0.9 %copy-done = bf16[256,4,128]{2,1,0:T(4,128)(2,1)S(1)} copy-done((bf16[256,4,128]{2,1,0:T(4,128)(2,1)S(1)}, bf16[256,4,128]{2,1,0:T(4,128)(2,1)}, u32[]{:S(2)}) %copy-start) | copy-done | bytes 262168
  1.6 0.0 copy-start.1
  1.6 0.8 %copy-done.1 = s32[3,2048]{1,0:T(4,128)S(1)} copy-done((s32[3,2048]{1,0:T(4,128)S(1)}, s32[3,2048]{1,0:T(4,128)}, u32[]{:S(2)}) %copy-start.1) | copy-done | bytes 24600
  2.3 0.0 copy-start.2
  2.3 0.7 %copy-done.2 = bf16[16,256]{1,0:T(8,128)(2,1)S(1)} copy-done((bf16[16,256]{1,0:T(8,128)(2,1)S(1)}, bf16[16,256]{1,0:T(8,128)(2,1)}, u32[]{:S(2)}) %copy-start.2) | copy-done | bytes 8216
  3.0 60.7 %window.1 = (f32[1,16,128,256]{3,2,1,0:T(8,128)S(1)}, f32[1,16,128,256]{3,2,1,0:T(8,128)S(1)}) custom-call(bf16[1024,128]{1,0:T(8,128)(2,1)S(1)} %bitcast.1, bf16[16,256]{1,0:T(8,128)(2,1)S(1)} %copy-done.2, s32[3,2048]{1,0:T(4,128)S(1)} %copy-done.1, f32[16,128,256]{2,1,0:T(8,128)} %vt_hbm.1, f32[1,16,128,256]{3,2,1,0:T(8,128)} %before_hbm.1, ...), custom_call_target="tpu_custom_call" | custom-call | tf_op jit(solution)/shard_map/window/pallas_call | solution.py:334
  63.7 1.3 %copy.10 = f32[1,16,128,256]{3,2,1,0:T(8,128)} copy(f32[1,16,128,256]{3,2,1,0:T(8,128)S(1)} %get-tuple-element.4) | data formatting | bytes 4194304
  65.1 1.3 %copy.11 = f32[1,16,128,256]{3,2,1,0:T(8,128)} copy(f32[1,16,128,256]{3,2,1,0:T(8,128)S(1)} %get-tuple-element.5) | data formatting | bytes 4194304
Async XLA Ops:
  0.6 1.0 %copy-start = (bf16[256,4,128]{2,1,0:T(4,128)(2,1)S(1)}, bf16[256,4,128]{2,1,0:T(4,128)(2,1)}, u32[]{:S(2)}) copy-start(bf16[256,4,128]{2,1,0:T(4,128)(2,1)} %param.6) | copy-start | bytes 786436
  1.6 0.8 %copy-start.1 = (s32[3,2048]{1,0:T(4,128)S(1)}, s32[3,2048]{1,0:T(4,128)}, u32[]{:S(2)}) copy-start(s32[3,2048]{1,0:T(4,128)} %cells_hbm.1) | copy-start | bytes 73732
  2.3 0.7 %copy-start.2 = (bf16[16,256]{1,0:T(8,128)(2,1)S(1)}, bf16[16,256]{1,0:T(8,128)(2,1)}, u32[]{:S(2)}) copy-start(bf16[16,256]{1,0:T(8,128)(2,1)} %enc_hbm.1) | copy-start | bytes 24580

commit v2 on v1

v2 whole, which is shorter than its diff:
```python
import functools

import jax
import jax.numpy as jnp
from jax import lax
from jax.experimental import pallas as pl
from jax.experimental.pallas import tpu as pltpu
from jax.sharding import PartitionSpec as P

C0, C1, C2, C3, C4 = (-205.0 / 72.0, 8.0 / 5.0, -1.0 / 5.0, 8.0 / 315.0, -1.0 / 560.0)
SCALE = 5040.0
BAND = (8064.0, -1008.0, 128.0, -9.0)
MESH = pl.DeviceIdType.MESH
F32 = jnp.float32
BF16 = jnp.bfloat16


def band_of(distance):
    value = jnp.zeros(distance.shape, F32)
    for j, weight in enumerate(BAND, 1):
        value = jnp.where(distance == j, weight, value)
    return value.astype(BF16)


def iota(shape, dim):
    return lax.broadcasted_iota(jnp.int32, shape, dim)


def split(value):
    high = value.astype(BF16)
    return high, (value - high.astype(F32)).astype(BF16)


def dot(a, b):
    return jnp.dot(a, b, preferred_element_type=F32)


def kernel(
    n_grid, n_shot, res_hbm, enc_hbm, cells_hbm, vt_hbm, before_hbm, start_hbm, fa, fb,
    vt, halo, stage, zmat, ymat, res, enc, cells, part, other, full, shots, traces, oy, oxz, inj,
    load_sem, send_sem, recv_sem, pair_sem, block_send, block_recv, shot_send, shot_recv, row_send, row_recv, ready,
):
    g = lax.axis_index("grid")
    s = lax.axis_index("shot")
    width, rows, depth = vt.shape
    half = depth // 2
    even = lax.rem(g, 2) == 0
    odd = lax.rem(g, 2) == 1
    has = (g > 0, g < n_grid - 1)
    near = (jnp.maximum(g - 1, 0), jnp.minimum(g + 1, n_grid - 1))
    place = lax.rem(g, 4)
    row = g // 4
    n_rows = n_grid // 4
    flipped = g + jnp.where(place < 2, 2, -2)

    def mate(k):
        return {"grid": jnp.where(lax.rem(k, 2) == lax.rem(s, 2), g, flipped), "shot": k}

    loads = [
        pltpu.make_async_copy(src, dst, load_sem.at[i])
        for i, (src, dst) in enumerate((
            (res_hbm, res),
            (enc_hbm, enc),
            (start_hbm.at[0], fb.at[pl.ds(4, width)]),
            (before_hbm.at[0], fa.at[pl.ds(4, width)]),
            (vt_hbm, vt),
            (cells_hbm, cells),
        ))
    ]
    for load in loads:
        load.start()

    barrier = pltpu.get_barrier_semaphore()

    def greet(**device):
        pl.semaphore_signal(barrier, inc=1, device_id=device, device_id_type=MESH)

    @pl.when(even)
    def _():
        greet(grid=near[1])

        @pl.when(has[0])
        def _():
            greet(grid=near[0])

        for i in range(1, n_shot):
            greet(**mate(lax.rem(s + i, n_shot)))
        for i in range(1, n_rows):
            greet(grid=lax.rem(g + 4 * i, n_grid))

    @pl.when(odd)
    def _():
        for i in range(n_rows):
            greet(grid=lax.rem(g - 1 + 4 * i, n_grid))

    zmat[...] = band_of(jnp.abs(iota((depth, depth), 0) - iota((depth, depth), 1)))
    ymat[...] = band_of(jnp.abs(iota((rows, 2 * rows), 0) - lax.rem(iota((rows, 2 * rows), 1), rows)))
    for f in (fa, fb):
        for p in (0, width + 4):
            f[pl.ds(p, 4)] = jnp.zeros((4, rows, depth), F32)

    def halo_copy(n, side, h, src):
        lanes = pl.ds(h * half, half)
        return pltpu.make_async_remote_copy(
            src_ref=stage.at[side] if (n, h) == (1, 0) else src.at[:, :, lanes],
            dst_ref=halo.at[n, 1 - side, :, :, lanes],
            send_sem=send_sem.at[n, side, h],
            recv_sem=recv_sem.at[n, 1 - side, h],
            device_id={"grid": near[side]},
            device_id_type=MESH,
        )

    def edge_of(n, side):
        if n == 0:
            return start_hbm.at[0, pl.ds(0 if side == 0 else width - 4, 4)]
        f = fb if n % 2 == 0 else fa
        return f.at[pl.ds(4 if side == 0 else width, 4)]

    def send_halo(n, side, h):
        @pl.when(has[side])
        def _():
            halo_copy(n, side, h, edge_of(n, side)).start()

    def wait_sent(n):
        for side in (0, 1):
            @pl.when(has[side])
            def _():
                for h in (1, 0):
                    halo_copy(n, side, h, edge_of(n, side)).wait_send()

    def pair_copy(target):
        return pltpu.make_async_remote_copy(
            src_ref=part, dst_ref=other, send_sem=pair_sem.at[0], recv_sem=pair_sem.at[1],
            device_id={"grid": target}, device_id_type=MESH,
        )

    def block_copy(y, sem, target):
        rows_of = full.at[:, pl.ds(8 * y, 8)]
        return pltpu.make_async_remote_copy(
            src_ref=rows_of, dst_ref=rows_of, send_sem=block_send.at[sem], recv_sem=block_recv.at[y],
            device_id={"grid": target}, device_id_type=MESH,
        )

    loads[0].wait()
    loads[1].wait()
    shot_rows, samples = res.shape[0] // 4, 4
    core = lax.rem(g, 2)
    r = iota((8 * n_shot, n_shot), 0)
    pick = jnp.where(r // 8 == iota((8 * n_shot, n_shot), 1), 1.0, 0.0).astype(BF16)
    spread = jnp.where(
        iota((shot_rows, 4 * shot_rows), 0) == iota((shot_rows, 4 * shot_rows), 1) // 4, 1.0, 0.0
    ).astype(BF16)
    weights = dot(dot(pick, enc[...]).astype(BF16), spread)
    wide = (8 * n_shot, 4 * shot_rows)
    weights = jnp.where(lax.rem(iota(wide, 0), 8) - 4 * core == lax.rem(iota(wide, 1), 4), weights, 0.0)
    part[...] = dot(weights.astype(BF16), res[...]).reshape(n_shot, 8, 128)

    @pl.when(odd)
    def _():
        pl.semaphore_wait(barrier, jnp.where(has[1], 2, 1))
        for side in (0, 1):
            @pl.when(has[side])
            def _():
                pl.semaphore_signal(ready.at[1 - side], inc=1, device_id={"grid": near[side]}, device_id_type=MESH)

    for side in (1, 0):
        @pl.when(even & has[side])
        def _():
            pl.semaphore_wait(ready.at[side], 1)
    @pl.when(place == 0)
    def _():
        pair_copy(near[1]).start()

    @pl.when(place == 3)
    def _():
        pair_copy(near[0]).start()

    over_y = (place == 2, place == 1)
    for h in (1, 0):
        for side in (0, 1):
            @pl.when(jnp.logical_not(over_y[side]))
            def _():
                send_halo(0, side, h)

    @pl.when(place == 1)
    def _():
        pair_copy(near[0]).wait_recv()
        full[:, pl.ds(0, 8)] = part[...] + other[...]
        block_copy(0, 0, near[1]).start()
        block_copy(0, 1, near[0]).start()

    @pl.when(place == 2)
    def _():
        pair_copy(near[1]).wait_recv()
        full[:, pl.ds(8, 8)] = part[...] + other[...]
        block_copy(1, 0, near[0]).start()

    for h in (1, 0):
        for side in (0, 1):
            @pl.when(over_y[side])
            def _():
                send_halo(0, side, h)

    for load in loads[2:]:
        load.wait()

    n_rec = cells.shape[1]
    oy[...] = jnp.where(iota((rows, n_rec), 0) == cells[1:2, :], 1.0, 0.0).astype(BF16)
    spot = (cells[0:1, :] - g * width + 8) * 8 + cells[2:3, :]
    oxz[...] = jnp.where(iota(oxz.shape, 0) == spot, 1.0, 0.0).astype(BF16)

    def own_part(n, lanes=pl.ds(0, depth)):
        cur, nxt = (fb, fa) if n % 2 == 0 else (fa, fb)

        def plane(x, carry):
            high, low = split(cur[x + 4])
            along = zmat[:, lanes]
            across = dot(jnp.concatenate([high, low], axis=1), jnp.concatenate([along, along], axis=0))
            at = slice(lanes.start, lanes.start + lanes.size)
            across = across + dot(ymat[...], jnp.concatenate([high[:, at], low[:, at]], axis=0))
            u = cur[x + 4, :, lanes]
            total = (3.0 * C0) * u + across * (1.0 / SCALE)
            for j, weight in enumerate((C1, C2, C3, C4), 1):
                total = total + weight * (cur[x + 4 + j, :, lanes] + cur[x + 4 - j, :, lanes])
            nxt[x + 4, :, lanes] = 2.0 * u - nxt[x + 4, :, lanes] + vt[x, :, lanes] * total
            return carry

        lax.fori_loop(0, width, plane, 0)

    def add_halo(n, side, h):
        nxt = fa if n % 2 == 0 else fb
        lanes = pl.ds(h * half, half)

        @pl.when(has[side])
        def _():
            halo_copy(n, 1 - side, h, edge_of(n, 1 - side)).wait_recv()
            if (n, h) == (1, 0):
                for p in range(4):
                    x = p - 4 if side == 0 else width + p
                    halo[n, side, p, :, lanes] = halo[n, side, p, :, lanes] + traces_at(0, x)
            layer = [halo[n, side, 4 - d if side == 0 else d - 1, :, lanes] for d in (1, 2, 3, 4)]
            for i in range(4):
                x = i if side == 0 else width - 1 - i
                total = C4 * layer[3 - i]
                for j, weight in ((1, C1), (2, C2), (3, C3)):
                    if j > i:
                        total = total + weight * layer[j - i - 1]
                value = nxt[x + 4, :, lanes] + vt[x, :, lanes] * total
                nxt[x + 4, :, lanes] = value
                if (n, h) == (0, 0):
                    stage[side, i if side == 0 else 3 - i] = value

    def traces_at(n, x):
        tile, lane = divmod(8 * (x + 8), half)
        values = inj[3 - n, :, pl.ds(tile * half, half)]
        moved = values if lane == 0 else pltpu.roll(values, half - lane, 1)
        return jnp.where(iota((rows, half), 1) < 8, moved, 0.0)

    def inject(n, planes):
        nxt = fa if n % 2 == 0 else fb
        for x in planes:
            nxt[x + 4, :, pl.ds(0, half)] = nxt[x + 4, :, pl.ds(0, half)] + traces_at(n, x)

    edges = list(range(4)) + list(range(width - 4, width))
    inner = list(range(4, width - 4))

    own_part(0)

    def shot_copy(k):
        return pltpu.make_async_remote_copy(
            src_ref=full.at[k], dst_ref=shots.at[s], send_sem=shot_send.at[k], recv_sem=shot_recv.at[s],
            device_id=mate(k), device_id_type=MESH,
        )

    def shot_arrival(k):
        return pltpu.make_async_remote_copy(
            src_ref=full.at[k], dst_ref=shots.at[k], send_sem=shot_send.at[k], recv_sem=shot_recv.at[k],
            device_id=mate(k), device_id_type=MESH,
        )

    def row_copy(i, core):
        return pltpu.make_async_remote_copy(
            src_ref=traces.at[row], dst_ref=traces.at[row], send_sem=row_send.at[i, core], recv_sem=row_recv.at[row],
            device_id={"grid": lax.rem(g + 4 * i + core, n_grid)}, device_id_type=MESH,
        )

    def row_arrival(i):
        return pltpu.make_async_remote_copy(
            src_ref=traces.at[i], dst_ref=traces.at[i], send_sem=row_send.at[0, 0], recv_sem=row_recv.at[i],
            device_id={"grid": near[0]}, device_id_type=MESH,
        )

    row_targets = [(i, core) for i in range(n_rows) for core in (0, 1) if i or core]

    @pl.when(place == 1)
    def _():
        block_copy(1, 2, near[1]).wait_recv()
        block_copy(1, 2, near[0]).start()

    @pl.when(place == 0)
    def _():
        block_copy(0, 0, near[1]).wait_recv()
        block_copy(1, 0, near[1]).wait_recv()

    @pl.when(place == 2)
    def _():
        block_copy(0, 0, near[0]).wait_recv()

    @pl.when(even)
    def _():
        shots[s] = full[s]
        pl.semaphore_wait(barrier, n_shot - 1 + 2 * n_rows - 1)
        for i in range(1, n_shot):
            shot_copy(lax.rem(s + i, n_shot)).start()

    for side in (0, 1):
        add_halo(0, side, 1)
        send_halo(1, side, 1)

    @pl.when(even)
    def _():
        for i in range(1, n_shot):
            shot_arrival(lax.rem(s + i, n_shot)).wait_recv()
        traces[row] = jnp.sum(shots[...], axis=0)
        for target in row_targets:
            row_copy(*target).start()

    for side in (0, 1):
        add_halo(0, side, 0)
        send_halo(1, side, 0)

    own_part(1, pl.ds(half, half))
    for side in (0, 1):
        add_halo(1, side, 1)
        send_halo(2, side, 1)

    for i in range(n_rows):
        @pl.when(jnp.logical_not(even & (row == i)))
        def _():
            row_arrival(i).wait_recv()

    for t in (3, 2, 1, 0):
        values = jnp.concatenate([traces[i // 4, pl.ds(4 * (i % 4) + t, 1), :] for i in range(n_grid)], axis=1)
        total = jnp.zeros((rows, oxz.shape[0]), F32)
        for piece in split(values):
            scaled = oy[...] * jnp.broadcast_to(piece, oy.shape)
            total = total + lax.dot_general(scaled, oxz[...], (((1,), (1,)), ((), ())), preferred_element_type=F32)
        inj[t] = total

    inject(0, edges + inner)
    own_part(1, pl.ds(0, half))
    inject(1, edges)
    for side in (0, 1):
        add_halo(1, side, 0)
        send_halo(2, side, 0)
    inject(1, inner)

    for n in (2, 3):
        wait_sent(n - 1)
        own_part(n)
        inject(n, edges + inner)
        for h in (1, 0):
            for side in (0, 1):
                add_halo(n, side, h)
                if n < 3:
                    send_halo(n + 1, side, h)

    wait_sent(0)
    wait_sent(3)

    @pl.when(place == 0)
    def _():
        pair_copy(near[1]).wait_send()

    @pl.when(place == 3)
    def _():
        pair_copy(near[0]).wait_send()

    @pl.when(place == 1)
    def _():
        block_copy(0, 0, near[1]).wait_send()
        block_copy(0, 1, near[0]).wait_send()
        block_copy(1, 2, near[0]).wait_send()

    @pl.when(place == 2)
    def _():
        block_copy(1, 0, near[0]).wait_send()

    @pl.when(even)
    def _():
        for i in range(1, n_shot):
            shot_copy(lax.rem(s + i, n_shot)).wait_send()
        for target in row_targets:
            row_copy(*target).wait_send()


def local(n_grid, n_shot, residuals, encoding, receiver_cells, velocity_term, field_before, field_start):
    shot_rows, samples, local_receivers = residuals.shape
    width, rows, depth = velocity_term.shape
    flat = residuals.reshape(shot_rows * samples, local_receivers)
    n_rec = receiver_cells.shape[1]
    dma = pltpu.SemaphoreType.DMA
    padded = (width + 8, rows, depth)
    vmem = pl.BlockSpec(memory_space=pltpu.VMEM)
    hbm = [
        pltpu.with_memory_space_constraint(a, pltpu.HBM)
        for a in (flat, encoding, receiver_cells, velocity_term, field_before, field_start)
    ]
    fields = pl.pallas_call(
        functools.partial(kernel, n_grid, n_shot),
        out_shape=(pltpu.VMEM(padded, F32), pltpu.VMEM(padded, F32)),
        in_specs=[pl.BlockSpec(memory_space=pltpu.HBM)] * 6,
        out_specs=(vmem, vmem),
        scratch_shapes=[
            pltpu.VMEM((width, rows, depth), F32),
            pltpu.VMEM((4, 2, 4, rows, depth), F32),
            pltpu.VMEM((2, 4, rows, depth // 2), F32),
            pltpu.VMEM((depth, depth), BF16),
            pltpu.VMEM((rows, 2 * rows), BF16),
            pltpu.VMEM(flat.shape, BF16),
            pltpu.VMEM(encoding.shape, BF16),
            pltpu.VMEM(receiver_cells.shape, jnp.int32),
            pltpu.VMEM((n_shot, 8, local_receivers), F32),
            pltpu.VMEM((n_shot, 8, local_receivers), F32),
            pltpu.VMEM((n_shot, 16, local_receivers), F32),
            pltpu.VMEM((n_shot, 16, local_receivers), F32),
            pltpu.VMEM((n_grid // 4, 16, local_receivers), F32),
            pltpu.VMEM((rows, n_rec), BF16),
            pltpu.VMEM((8 * (width + 16), n_rec), BF16),
            pltpu.VMEM((4, rows, 8 * (width + 16)), F32),
            dma((6,)),
            dma((4, 2, 2)),
            dma((4, 2, 2)),
            dma((2,)),
            dma((3,)),
            dma((2,)),
            dma((n_shot,)),
            dma((n_shot,)),
            dma((n_grid // 4, 2)),
            dma((n_grid // 4,)),
            pltpu.SemaphoreType.REGULAR((2,)),
        ],
        compiler_params=pltpu.CompilerParams(
            collective_id=0, has_side_effects=True, vmem_limit_bytes=40 * 1024 * 1024
        ),
        name="window",
    )(*hbm)

    def flush(fa, fb, last, end, sem):
        copies = []
        for i, (field, out) in enumerate(((fa, last), (fb, end))):
            for j in range(4):
                size = width // 4
                copies.append(pltpu.make_async_copy(
                    field.at[pl.ds(4 + j * size, size)], out.at[0, pl.ds(j * size, size)], sem.at[i, j]
                ))
        for copy in copies:
            copy.start()
        for copy in copies:
            copy.wait()

    field = jax.ShapeDtypeStruct(field_start.shape, F32)
    return pl.pallas_call(
        flush,
        out_shape=(field, field),
        in_specs=[vmem, vmem],
        out_specs=[pl.BlockSpec(memory_space=pltpu.HBM)] * 2,
        scratch_shapes=[dma((2, 4))],
        compiler_params=pltpu.CompilerParams(vmem_limit_bytes=16 * 1024 * 1024),
        name="flush",
    )(*fields)


def solution(mesh):
    return jax.shard_map(
        functools.partial(local, mesh.shape["grid"], mesh.shape["shot"]),
        mesh=mesh,
        in_specs=(
            P("shot", None, "grid"),
            P(None, "shot"),
            P(),
            P("grid", None, None),
            P("shot", "grid", None, None),
            P("shot", "grid", None, None),
        ),
        out_specs=(P("shot", "grid", None, None), P("shot", "grid", None, None)),
        check_vma=False,
    )
```

time: 66.6 us -> 59.3 us (0.89)
  local copies, waits for them, and re-layouts: 5.04 us -> 0 us
  Pallas kernels: 60.7 us -> 58.5 us
    unnamed x8 -> x0, local copies, waits for them, and re-layouts: 5.04 us -> none
    pallas_call x1 -> x2, Pallas kernels: 60.7 us -> 58.5 us  [the longest x1 56.5 us: local(): pl.pallas_call(functools.partial(kernel, n_grid, n_shot), out_shape=(pltp...]
where the time goes in v2:
time: 59.3 us; the launch traced here: 59.2 us
  Pallas kernels  58.5 us (99%)
  between operations  0.64 us (1%)
    pallas_call x1, Pallas kernels, local(): pl.pallas_call(functools.partial(kernel, n_grid, n_shot), out_shape=(pltp...  56.5 us
    pallas_call x1, Pallas kernels, local(): pl.pallas_call(flush, out_shape=(field, field), in_specs=[vmem, vmem], ou...  2.07 us

profile of v2, /device:TPU:1, one launch (start us, length us, event | category | flops | bytes accessed | tf_op | source)
XLA Modules:
  0.0 59.2 jit_solution(11700435815951003305)
XLA Ops:
  0.6 56.5 %window.1 = (f32[24,128,256]{2,1,0:T(8,128)S(1)}, f32[24,128,256]{2,1,0:T(8,128)S(1)}) custom-call(bf16[1024,128]{1,0:T(8,128)(2,1)} %bitcast.1, bf16[16,256]{1,0:T(8,128)(2,1)} %enc_hbm.1, s32[3,2048]{1,0:T(4,128)} %cells_hbm.1, f32[16,128,256]{2,1,0:T(8,128)} %vt_hbm.1, f32[1,16,128,256]{3,2,1,0:T(8,128)} %before_hbm.1, f32[1,16,128,256]{3,2,1,0:T(8,128)} %start_hbm.1), custom_call_target="tpu_custom_call" | custom-call | tf_op jit(solution)/shard_map/window/pallas_call | solution.py:409
  57.1 2.1 %flush.1 = (f32[1,16,128,256]{3,2,1,0:T(8,128)}, f32[1,16,128,256]{3,2,1,0:T(8,128)}) custom-call(f32[24,128,256]{2,1,0:T(8,128)S(1)} %get-tuple-element.4.fa, f32[24,128,256]{2,1,0:T(8,128)S(1)} %get-tuple-element.5.fb), custom_call_target="tpu_custom_call" | custom-call | tf_op jit(solution)/shard_map/flush/pallas_call | solution.py:463

commit v3 on v2

--- a/solution.py
+++ b/solution.py
@@ -38,7 +38,7 @@
 def kernel(
     n_grid, n_shot, res_hbm, enc_hbm, cells_hbm, vt_hbm, before_hbm, start_hbm, fa, fb,
     vt, halo, stage, zmat, ymat, res, enc, cells, part, other, full, shots, traces, oy, oxz, inj,
-    load_sem, send_sem, recv_sem, pair_sem, block_send, block_recv, shot_send, shot_recv, row_send, row_recv, ready,
+    relay, load_sem, send_sem, recv_sem, relay_recv, relay_send, pair_sem, block_send, block_recv, shot_send, shot_recv, row_send, row_recv, ready, known,
 ):
     g = lax.axis_index("grid")
     s = lax.axis_index("shot")
@@ -116,10 +116,85 @@
         f = fb if n % 2 == 0 else fa
         return f.at[pl.ds(4 if side == 0 else width, 4)]
 
+    strip = rows // n_rows
+    by_relay = (row, n_rows - 1 - row)
+    diagonal = (place == 0, place == 3)
+    relay_at = (jnp.minimum(g + 2, n_grid - 1), jnp.maximum(g - 2, 0))
+
+    def source_of(n, side, h, p):
+        at = pl.ds(p * strip, strip)
+        if (n, h) == (1, 0):
+            return stage.at[side, :, at]
+        return edge_of(n, side).at[:, at, pl.ds(h * half, half)]
+
+    def direct_piece(n, side, h, p):
+        return pltpu.make_async_remote_copy(
+            src_ref=source_of(n, side, h, p),
+            dst_ref=halo.at[n, 1 - side, :, pl.ds(p * strip, strip), pl.ds(h * half, half)],
+            send_sem=send_sem.at[n, side, h],
+            recv_sem=recv_sem.at[n, 1 - side, h],
+            device_id={"grid": near[side]},
+            device_id_type=MESH,
+        )
+
+    def relay_piece(n, side, h, p):
+        return pltpu.make_async_remote_copy(
+            src_ref=source_of(n, side, h, p),
+            dst_ref=relay.at[n, h, p],
+            send_sem=send_sem.at[n, side, h],
+            recv_sem=relay_recv.at[n, h, p],
+            device_id={"grid": relay_at[side]},
+            device_id_type=MESH,
+        )
+
+    def onward_piece(n, side, h, p):
+        target = jnp.maximum(g - 3, 0) if side == 0 else jnp.minimum(g + 3, n_grid - 1)
+        return pltpu.make_async_remote_copy(
+            src_ref=relay.at[n, h, p],
+            dst_ref=halo.at[n, 1 - side, :, pl.ds(p * strip, strip), pl.ds(h * half, half)],
+            send_sem=relay_send.at[n, h, p],
+            recv_sem=recv_sem.at[n, 1 - side, h],
+            device_id={"grid": target},
+            device_id_type=MESH,
+        )
+
+    def each_onward(n, h, act):
+        for side in (0, 1):
+            @pl.when(place == 2 - side)
+            def _():
+                for p in range(n_rows - 1):
+                    @pl.when(p < by_relay[side])
+                    def _():
+                        act(n, side, h, p)
+
+    def forward(n, h):
+        def act(n, side, h, p):
+            relay_piece(n, side, h, p).wait_recv()
+            onward_piece(n, side, h, p).start()
+
+        each_onward(n, h, act)
+
+    def send_direct(n, side, h):
+        for p in range(n_rows):
+            @pl.when(p >= by_relay[side])
+            def _():
+                direct_piece(n, side, h, p).start()
+
+    def send_by_relay(n, side, h):
+        for p in range(n_rows - 1):
+            @pl.when(p < by_relay[side])
+            def _():
+                relay_piece(n, side, h, p).start()
+
     def send_halo(n, side, h):
-        @pl.when(has[side])
+        @pl.when(has[side] & jnp.logical_not(diagonal[side]))
         def _():
             halo_copy(n, side, h, edge_of(n, side)).start()
+
+        @pl.when(has[side] & diagonal[side])
+        def _():
+            send_by_relay(n, side, h)
+            send_direct(n, side, h)
 
     def wait_sent(n):
         for side in (0, 1):
@@ -175,12 +250,30 @@
     def _():
         pair_copy(near[0]).start()
 
+    @pl.when(place == 2)
+    def _():
+        pl.semaphore_signal(known, inc=1, device_id={"grid": near[1]}, device_id_type=MESH)
+
     over_y = (place == 2, place == 1)
     for h in (1, 0):
         for side in (0, 1):
-            @pl.when(jnp.logical_not(over_y[side]))
+            @pl.when(jnp.logical_not(over_y[side] | ((place == 3) & (side == 1))))
             def _():
                 send_halo(0, side, h)
+
+    @pl.when(place == 3)
+    def _():
+        @pl.when(has[1])
+        def _():
+            send_direct(0, 1, 1)
+
+        pl.semaphore_wait(known, 1)
+
+        @pl.when(has[1])
+        def _():
+            send_by_relay(0, 1, 1)
+            send_direct(0, 1, 0)
+            send_by_relay(0, 1, 0)
 
     @pl.when(place == 1)
     def _():
@@ -313,9 +406,11 @@
         for i in range(1, n_shot):
             shot_copy(lax.rem(s + i, n_shot)).start()
 
+    forward(0, 1)
     for side in (0, 1):
         add_halo(0, side, 1)
         send_halo(1, side, 1)
+    forward(0, 0)
 
     @pl.when(even)
     def _():
@@ -330,9 +425,11 @@
         send_halo(1, side, 0)
 
     own_part(1, pl.ds(half, half))
+    forward(1, 1)
     for side in (0, 1):
         add_halo(1, side, 1)
         send_halo(2, side, 1)
+    forward(1, 0)
 
     for i in range(n_rows):
         @pl.when(jnp.logical_not(even & (row == i)))
@@ -360,12 +457,16 @@
         own_part(n)
         inject(n, edges + inner)
         for h in (1, 0):
+            forward(n, h)
             for side in (0, 1):
                 add_halo(n, side, h)
                 if n < 3:
                     send_halo(n + 1, side, h)
 
     wait_sent(0)
+    for n in range(4):
+        for h in (1, 0):
+            each_onward(n, h, lambda *which: onward_piece(*which).wait_send())
     wait_sent(3)
 
     @pl.when(place == 0)
@@ -428,9 +529,12 @@
             pltpu.VMEM((rows, n_rec), BF16),
             pltpu.VMEM((8 * (width + 16), n_rec), BF16),
             pltpu.VMEM((4, rows, 8 * (width + 16)), F32),
+            pltpu.VMEM((4, 2, n_grid // 4 - 1, 4, rows // (n_grid // 4), depth // 2), F32),
             dma((6,)),
             dma((4, 2, 2)),
             dma((4, 2, 2)),
+            dma((4, 2, n_grid // 4 - 1)),
+            dma((4, 2, n_grid // 4 - 1)),
             dma((2,)),
             dma((3,)),
             dma((2,)),
@@ -439,6 +543,7 @@
             dma((n_grid // 4, 2)),
             dma((n_grid // 4,)),
             pltpu.SemaphoreType.REGULAR((2,)),
+            pltpu.SemaphoreType.REGULAR,
         ],
         compiler_params=pltpu.CompilerParams(
             collective_id=0, has_side_effects=True, vmem_limit_bytes=40 * 1024 * 1024

time: 59.3 us -> 58.2 us (0.981)
  the two profiles are of different devices: /device:TPU:1 before, /device:TPU:4 now
where the time goes in v3:
time: 58.2 us; the launch traced here: 58.1 us
  Pallas kernels  57.4 us (99%)
  between operations  0.64 us (1%)
    pallas_call x1, Pallas kernels, local(): pl.pallas_call(functools.partial(kernel, n_grid, n_shot), out_shape=(pltp...  55.4 us
    pallas_call x1, Pallas kernels, local(): pl.pallas_call(flush, out_shape=(field, field), in_specs=[vmem, vmem], ou...  2.07 us

profile of v3, /device:TPU:4, one launch (start us, length us, event | category | flops | bytes accessed | tf_op | source)
XLA Modules:
  0.0 58.1 jit_solution(12615006655565501283)
XLA Ops:
  0.6 55.4 %window.1 = (f32[24,128,256]{2,1,0:T(8,128)S(1)}, f32[24,128,256]{2,1,0:T(8,128)S(1)}) custom-call(bf16[1024,128]{1,0:T(8,128)(2,1)} %bitcast.1, bf16[16,256]{1,0:T(8,128)(2,1)} %enc_hbm.1, s32[3,2048]{1,0:T(4,128)} %cells_hbm.1, f32[16,128,256]{2,1,0:T(8,128)} %vt_hbm.1, f32[1,16,128,256]{3,2,1,0:T(8,128)} %before_hbm.1, f32[1,16,128,256]{3,2,1,0:T(8,128)} %start_hbm.1), custom_call_target="tpu_custom_call" | custom-call | tf_op jit(solution)/shard_map/window/pallas_call | solution.py:510
  56.0 2.1 %flush.1 = (f32[1,16,128,256]{3,2,1,0:T(8,128)}, f32[1,16,128,256]{3,2,1,0:T(8,128)}) custom-call(f32[24,128,256]{2,1,0:T(8,128)S(1)} %get-tuple-element.4.fa, f32[24,128,256]{2,1,0:T(8,128)S(1)} %get-tuple-element.5.fb), custom_call_target="tpu_custom_call" | custom-call | tf_op jit(solution)/shard_map/flush/pallas_call | solution.py:568

commit v4 on v3

--- a/solution.py
+++ b/solution.py
@@ -196,12 +196,15 @@
             send_by_relay(n, side, h)
             send_direct(n, side, h)
 
+    def wait_half_sent(n, side, h):
+        @pl.when(has[side])
+        def _():
+            halo_copy(n, side, h, edge_of(n, side)).wait_send()
+
     def wait_sent(n):
         for side in (0, 1):
-            @pl.when(has[side])
-            def _():
-                for h in (1, 0):
-                    halo_copy(n, side, h, edge_of(n, side)).wait_send()
+            for h in (1, 0):
+                wait_half_sent(n, side, h)
 
     def pair_copy(target):
         return pltpu.make_async_remote_copy(
@@ -255,11 +258,10 @@
         pl.semaphore_signal(known, inc=1, device_id={"grid": near[1]}, device_id_type=MESH)
 
     over_y = (place == 2, place == 1)
-    for h in (1, 0):
-        for side in (0, 1):
-            @pl.when(jnp.logical_not(over_y[side] | ((place == 3) & (side == 1))))
-            def _():
-                send_halo(0, side, h)
+    for side in (0, 1):
+        @pl.when(jnp.logical_not(over_y[side] | ((place == 3) & (side == 1))))
+        def _():
+            send_halo(0, side, 1)
 
     @pl.when(place == 3)
     def _():
@@ -272,8 +274,6 @@
         @pl.when(has[1])
         def _():
             send_by_relay(0, 1, 1)
-            send_direct(0, 1, 0)
-            send_by_relay(0, 1, 0)
 
     @pl.when(place == 1)
     def _():
@@ -288,19 +288,13 @@
         full[:, pl.ds(8, 8)] = part[...] + other[...]
         block_copy(1, 0, near[0]).start()
 
-    for h in (1, 0):
-        for side in (0, 1):
-            @pl.when(over_y[side])
-            def _():
-                send_halo(0, side, h)
+    for side in (0, 1):
+        @pl.when(over_y[side])
+        def _():
+            send_halo(0, side, 1)
 
     for load in loads[2:]:
         load.wait()
-
-    n_rec = cells.shape[1]
-    oy[...] = jnp.where(iota((rows, n_rec), 0) == cells[1:2, :], 1.0, 0.0).astype(BF16)
-    spot = (cells[0:1, :] - g * width + 8) * 8 + cells[2:3, :]
-    oxz[...] = jnp.where(iota(oxz.shape, 0) == spot, 1.0, 0.0).astype(BF16)
 
     def own_part(n, lanes=pl.ds(0, depth)):
         cur, nxt = (fb, fa) if n % 2 == 0 else (fa, fb)
@@ -358,6 +352,8 @@
     inner = list(range(4, width - 4))
 
     own_part(0)
+    for side in (0, 1):
+        send_halo(0, side, 0)
 
     def shot_copy(k):
         return pltpu.make_async_remote_copy(
@@ -406,11 +402,23 @@
         for i in range(1, n_shot):
             shot_copy(lax.rem(s + i, n_shot)).start()
 
+    n_rec = cells.shape[1]
+    oy[...] = jnp.where(iota((rows, n_rec), 0) == cells[1:2, :], 1.0, 0.0).astype(BF16)
+    spot = ((cells[0:1, :] - g * width + 8) * 8 + cells[2:3, :]).astype(F32)
+    spot = jnp.transpose(jnp.broadcast_to(spot, (128, n_rec)))
+    for tile in range(oxz.shape[1] // 128):
+        lane = (iota((n_rec, 128), 1) + 128 * tile).astype(F32)
+        oxz[:, pl.ds(128 * tile, 128)] = jnp.where(spot == lane, 1.0, 0.0).astype(BF16)
+
     forward(0, 1)
     for side in (0, 1):
         add_halo(0, side, 1)
         send_halo(1, side, 1)
     forward(0, 0)
+
+    for side in (0, 1):
+        add_halo(0, side, 0)
+        send_halo(1, side, 0)
 
     @pl.when(even)
     def _():
@@ -420,10 +428,6 @@
         for target in row_targets:
             row_copy(*target).start()
 
-    for side in (0, 1):
-        add_halo(0, side, 0)
-        send_halo(1, side, 0)
-
     own_part(1, pl.ds(half, half))
     forward(1, 1)
     for side in (0, 1):
@@ -436,14 +440,14 @@
         def _():
             row_arrival(i).wait_recv()
 
-    for t in (3, 2, 1, 0):
+    def build(t):
         values = jnp.concatenate([traces[i // 4, pl.ds(4 * (i % 4) + t, 1), :] for i in range(n_grid)], axis=1)
-        total = jnp.zeros((rows, oxz.shape[0]), F32)
-        for piece in split(values):
-            scaled = oy[...] * jnp.broadcast_to(piece, oy.shape)
-            total = total + lax.dot_general(scaled, oxz[...], (((1,), (1,)), ((), ())), preferred_element_type=F32)
-        inj[t] = total
-
+        scaled = [oy[...] * jnp.broadcast_to(piece, oy.shape) for piece in split(values)]
+        total = dot(jnp.concatenate(scaled, axis=0), oxz[...])
+        inj[t] = total[:rows] + total[rows:]
+
+    build(3)
+    build(2)
     inject(0, edges + inner)
     own_part(1, pl.ds(0, half))
     inject(1, edges)
@@ -451,6 +455,8 @@
         add_halo(1, side, 0)
         send_halo(2, side, 0)
     inject(1, inner)
+    build(1)
+    build(0)
 
     for n in (2, 3):
         wait_sent(n - 1)
@@ -527,7 +533,7 @@
             pltpu.VMEM((n_shot, 16, local_receivers), F32),
             pltpu.VMEM((n_grid // 4, 16, local_receivers), F32),
             pltpu.VMEM((rows, n_rec), BF16),
-            pltpu.VMEM((8 * (width + 16), n_rec), BF16),
+            pltpu.VMEM((n_rec, 8 * (width + 16)), BF16),
             pltpu.VMEM((4, rows, 8 * (width + 16)), F32),
             pltpu.VMEM((4, 2, n_grid // 4 - 1, 4, rows // (n_grid // 4), depth // 2), F32),
             dma((6,)),

time: 58.2 us -> 55 us (0.945)
  the two profiles are of different devices: /device:TPU:4 before, /device:TPU:1 now
where the time goes in v4:
time: 55 us; the launch traced here: 54.8 us
  Pallas kernels  54.2 us (99%)
  between operations  0.64 us (1%)
    pallas_call x1, Pallas kernels, local(): pl.pallas_call(functools.partial(kernel, n_grid, n_shot), out_shape=(pltp...  52.1 us
    pallas_call x1, Pallas kernels, local(): pl.pallas_call(flush, out_shape=(field, field), in_specs=[vmem, vmem], ou...  2.07 us

profile of v4, /device:TPU:1, one launch (start us, length us, event | category | flops | bytes accessed | tf_op | source)
XLA Modules:
  0.0 54.8 jit_solution(14032776017439688802)
XLA Ops:
  0.6 52.1 %window.1 = (f32[24,128,256]{2,1,0:T(8,128)S(1)}, f32[24,128,256]{2,1,0:T(8,128)S(1)}) custom-call(bf16[1024,128]{1,0:T(8,128)(2,1)} %bitcast.1, bf16[16,256]{1,0:T(8,128)(2,1)} %enc_hbm.1, s32[3,2048]{1,0:T(4,128)} %cells_hbm.1, f32[16,128,256]{2,1,0:T(8,128)} %vt_hbm.1, f32[1,16,128,256]{3,2,1,0:T(8,128)} %before_hbm.1, f32[1,16,128,256]{3,2,1,0:T(8,128)} %start_hbm.1), custom_call_target="tpu_custom_call" | custom-call | tf_op jit(solution)/shard_map/window/pallas_call | solution.py:516
  52.8 2.1 %flush.1 = (f32[1,16,128,256]{3,2,1,0:T(8,128)}, f32[1,16,128,256]{3,2,1,0:T(8,128)}) custom-call(f32[24,128,256]{2,1,0:T(8,128)S(1)} %get-tuple-element.4.fa, f32[24,128,256]{2,1,0:T(8,128)S(1)} %get-tuple-element.5.fb), custom_call_target="tpu_custom_call" | custom-call | tf_op jit(solution)/shard_map/flush/pallas_call | solution.py:574

commit v5 on v4

--- a/solution.py
+++ b/solution.py
@@ -296,7 +296,7 @@
     for load in loads[2:]:
         load.wait()
 
-    def own_part(n, lanes=pl.ds(0, depth)):
+    def own_part(n, planes, lanes=pl.ds(0, depth)):
         cur, nxt = (fb, fa) if n % 2 == 0 else (fa, fb)
 
         def plane(x, carry):
@@ -312,7 +312,11 @@
             nxt[x + 4, :, lanes] = 2.0 * u - nxt[x + 4, :, lanes] + vt[x, :, lanes] * total
             return carry
 
-        lax.fori_loop(0, width, plane, 0)
+        if planes is edges:
+            lax.fori_loop(0, 4, plane, 0)
+            lax.fori_loop(width - 4, width, plane, 0)
+        else:
+            lax.fori_loop(4, width - 4, plane, 0)
 
     def add_halo(n, side, h):
         nxt = fa if n % 2 == 0 else fb
@@ -351,7 +355,7 @@
     edges = list(range(4)) + list(range(width - 4, width))
     inner = list(range(4, width - 4))
 
-    own_part(0)
+    own_part(0, edges)
     for side in (0, 1):
         send_halo(0, side, 0)
 
@@ -414,6 +418,7 @@
     for side in (0, 1):
         add_halo(0, side, 1)
         send_halo(1, side, 1)
+    own_part(0, inner)
     forward(0, 0)
 
     for side in (0, 1):
@@ -428,11 +433,12 @@
         for target in row_targets:
             row_copy(*target).start()
 
-    own_part(1, pl.ds(half, half))
+    own_part(1, edges, pl.ds(half, half))
     forward(1, 1)
     for side in (0, 1):
         add_halo(1, side, 1)
         send_halo(2, side, 1)
+    own_part(1, inner, pl.ds(half, half))
     forward(1, 0)
 
     for i in range(n_rows):
@@ -449,25 +455,32 @@
     build(3)
     build(2)
     inject(0, edges + inner)
-    own_part(1, pl.ds(0, half))
+    own_part(1, edges, pl.ds(0, half))
     inject(1, edges)
     for side in (0, 1):
         add_halo(1, side, 0)
         send_halo(2, side, 0)
+    own_part(1, inner, pl.ds(0, half))
     inject(1, inner)
     build(1)
     build(0)
 
     for n in (2, 3):
         wait_sent(n - 1)
-        own_part(n)
-        inject(n, edges + inner)
+        own_part(n, edges)
+        inject(n, edges)
+        if n == 3:
+            own_part(n, inner)
+            inject(n, inner)
         for h in (1, 0):
             forward(n, h)
             for side in (0, 1):
                 add_halo(n, side, h)
                 if n < 3:
                     send_halo(n + 1, side, h)
+            if h == 1 and n < 3:
+                own_part(n, inner)
+                inject(n, inner)
 
     wait_sent(0)
     for n in range(4):

time: 55 us -> 53.2 us (0.967)
  Pallas kernels: 54.2 us -> 52 us
    pallas_call x1, Pallas kernels: 52.1 us -> 49.9 us  [local(): pl.pallas_call(functools.partial(kernel, n_grid, n_shot), out_shape=(pltp...]
where the time goes in v5:
time: 53.2 us; the launch traced here: 52.7 us
  Pallas kernels  52 us (98%)
  between operations  0.64 us (1%)
    pallas_call x1, Pallas kernels, local(): pl.pallas_call(functools.partial(kernel, n_grid, n_shot), out_shape=(pltp...  49.9 us
    pallas_call x1, Pallas kernels, local(): pl.pallas_call(flush, out_shape=(field, field), in_specs=[vmem, vmem], ou...  2.07 us

profile of v5, /device:TPU:1, one launch (start us, length us, event | category | flops | bytes accessed | tf_op | source)
XLA Modules:
  0.0 52.7 jit_solution(14655336429102612626)
XLA Ops:
  0.6 49.9 %window.1 = (f32[24,128,256]{2,1,0:T(8,128)S(1)}, f32[24,128,256]{2,1,0:T(8,128)S(1)}) custom-call(bf16[1024,128]{1,0:T(8,128)(2,1)} %bitcast.1, bf16[16,256]{1,0:T(8,128)(2,1)} %enc_hbm.1, s32[3,2048]{1,0:T(4,128)} %cells_hbm.1, f32[16,128,256]{2,1,0:T(8,128)} %vt_hbm.1, f32[1,16,128,256]{3,2,1,0:T(8,128)} %before_hbm.1, f32[1,16,128,256]{3,2,1,0:T(8,128)} %start_hbm.1), custom_call_target="tpu_custom_call" | custom-call | tf_op jit(solution)/shard_map/window/pallas_call | solution.py:529
  50.6 2.1 %flush.1 = (f32[1,16,128,256]{3,2,1,0:T(8,128)}, f32[1,16,128,256]{3,2,1,0:T(8,128)}) custom-call(f32[24,128,256]{2,1,0:T(8,128)S(1)} %get-tuple-element.4.fa, f32[24,128,256]{2,1,0:T(8,128)S(1)} %get-tuple-element.5.fb), custom_call_target="tpu_custom_call" | custom-call | tf_op jit(solution)/shard_map/flush/pallas_call | solution.py:587

commit v6 on v5

--- a/solution.py
+++ b/solution.py
@@ -462,22 +462,21 @@
         send_halo(2, side, 0)
     own_part(1, inner, pl.ds(0, half))
     inject(1, inner)
-    build(1)
-    build(0)
 
     for n in (2, 3):
         wait_sent(n - 1)
         own_part(n, edges)
-        inject(n, edges)
         if n == 3:
             own_part(n, inner)
-            inject(n, inner)
         for h in (1, 0):
             forward(n, h)
             for side in (0, 1):
                 add_halo(n, side, h)
                 if n < 3:
                     send_halo(n + 1, side, h)
+            if h == 1:
+                build(3 - n)
+                inject(n, edges if n < 3 else edges + inner)
             if h == 1 and n < 3:
                 own_part(n, inner)
                 inject(n, inner)

time: 53.2 us -> 53.1 us (level)
  no operation moved by 1% of the time
where the time goes in v6:
time: 53.1 us; the launch traced here: 52.5 us
  Pallas kernels  51.8 us (98%)
  between operations  0.64 us (1%)
    pallas_call x1, Pallas kernels, local(): pl.pallas_call(functools.partial(kernel, n_grid, n_shot), out_shape=(pltp...  49.8 us
    pallas_call x1, Pallas kernels, local(): pl.pallas_call(flush, out_shape=(field, field), in_specs=[vmem, vmem], ou...  2.07 us

profile of v6, /device:TPU:1, one launch (start us, length us, event | category | flops | bytes accessed | tf_op | source)
XLA Modules:
  0.0 52.5 jit_solution(8244067777703765995)
XLA Ops:
  0.6 49.8 %window.1 = (f32[24,128,256]{2,1,0:T(8,128)S(1)}, f32[24,128,256]{2,1,0:T(8,128)S(1)}) custom-call(bf16[1024,128]{1,0:T(8,128)(2,1)} %bitcast.1, bf16[16,256]{1,0:T(8,128)(2,1)} %enc_hbm.1, s32[3,2048]{1,0:T(4,128)} %cells_hbm.1, f32[16,128,256]{2,1,0:T(8,128)} %vt_hbm.1, f32[1,16,128,256]{3,2,1,0:T(8,128)} %before_hbm.1, f32[1,16,128,256]{3,2,1,0:T(8,128)} %start_hbm.1), custom_call_target="tpu_custom_call" | custom-call | tf_op jit(solution)/shard_map/window/pallas_call | solution.py:528
  50.4 2.1 %flush.1 = (f32[1,16,128,256]{3,2,1,0:T(8,128)}, f32[1,16,128,256]{3,2,1,0:T(8,128)}) custom-call(f32[24,128,256]{2,1,0:T(8,128)S(1)} %get-tuple-element.4.fa, f32[24,128,256]{2,1,0:T(8,128)S(1)} %get-tuple-element.5.fb), custom_call_target="tpu_custom_call" | custom-call | tf_op jit(solution)/shard_map/flush/pallas_call | solution.py:586
